TPU v7x, 256 devices: a whole 4x4x8 slice. The times are simulated.
256 devices in a mesh: wide: 64 (over z, x, core), narrow: 4 (over y).
Axes of the slice: x: 4, y: 4, z: 8, core: 2. Of those that a mesh axis runs over, the one named last changes fastest.
Arguments:
- coeffs: bfloat16 [2, 1024, 1024, 512], P(None, 'wide', None, 'narrow'), may hold values from -3 to 3
- legendre: bfloat16 [1024, 64, 1024], P('wide'), may hold values from -3 to 3
- order_table: int32 [1024], replicated, may hold values from 0 to 1023, each once
- thresholds: float32 [512], replicated, may hold values from 0.2 to 2
Outputs:
- lowrank: float32 [64, 2048, 512], P('wide', 'narrow')
- sparse: float32 [64, 2048, 512], P('wide', 'narrow')
Inputs may be any that keep to these rules, and one draw needn't show every extreme that they name: `order_table`: each order 0 to 1023 stands in exactly one slot.
All inputs are finite; a program needn't handle non-finite values.
Results may differ from a plain program's by a relative error of at most 0.0003.
Values sent between devices are 32-bit elements; how exact they have to be, the bound alone decides.
A program may use at most 128 MiB of HBM per device.

v0:
```python
import math
import jax
import jax.numpy as jnp
from jax import lax
from jax.sharding import PartitionSpec as P

NPIX = 2048
ITERS = 2


def soft_shrink(values, limits):
    return jnp.sign(values) * jnp.maximum(jnp.abs(values) - limits, 0.0)


def wiener_filter(covariance):
    chan_total = covariance.shape[0]
    ridge_shift = jnp.trace(covariance) / chan_total
    factor = jnp.linalg.cholesky(
        covariance + ridge_shift * jnp.eye(chan_total, dtype=covariance.dtype)
    )
    return jax.scipy.linalg.cho_solve((factor, True), covariance)


def per_device(coeffs, legendre, order_table, thresholds):
    slot_count = legendre.shape[0]
    degrees = legendre.shape[2]
    first_slot = lax.axis_index("wide") * slot_count
    own_orders = lax.dynamic_slice_in_dim(order_table, first_slot, slot_count)
    degree_mask = (
        lax.broadcasted_iota(jnp.int32, (slot_count, degrees), 1) >= own_orders[:, None]
    ).astype(legendre.dtype)
    masked = legendre * degree_mask[:, None, :]
    spectra = jnp.einsum("srl,kslc->ksrc", masked, coeffs, preferred_element_type=jnp.float32)
    pixels = lax.broadcasted_iota(jnp.int32, (1, NPIX), 1)
    pixel_phase = order_table[:, None] * pixels % NPIX
    pixel_angle = pixel_phase.astype(jnp.float32) * (2.0 * math.pi / NPIX)
    weights = jnp.where(order_table == 0, 1.0, 2.0).astype(jnp.float32)[:, None]
    cycle_table = jnp.stack([weights * jnp.cos(pixel_angle), -weights * jnp.sin(pixel_angle)])
    sky_map = jnp.einsum(
        "ksrc,ksj->rjc",
        lax.all_to_all(spectra, "wide", split_axis=2, concat_axis=1, tiled=True),
        cycle_table,
        precision=lax.Precision.HIGHEST,
        preferred_element_type=jnp.float32,
    )
    spectra_rows = lax.all_to_all(sky_map, "narrow", split_axis=1, concat_axis=2, tiled=True)
    cycle_count, pixel_count, chan_count = spectra_rows.shape
    sky_field = spectra_rows.reshape(cycle_count * pixel_count, chan_count)
    lowrank = jnp.zeros_like(sky_field)
    sparse = jnp.zeros_like(sky_field)
    for iteration in range(ITERS):
        sparse = soft_shrink(sky_field - lowrank, thresholds)
        residue = sky_field - sparse
        partial_cov = jnp.dot(
            residue.T, residue, precision=lax.Precision.HIGHEST, preferred_element_type=jnp.float32
        )
        covariance = lax.psum(partial_cov, ("wide", "narrow"))
        lowrank = jnp.dot(
            residue,
            wiener_filter(covariance),
            precision=lax.Precision.HIGHEST,
            preferred_element_type=jnp.float32,
        )
    return (
        lowrank.reshape(cycle_count, pixel_count, chan_count),
        sparse.reshape(cycle_count, pixel_count, chan_count),
    )


def solution(mesh):
    placed = (P(None, "wide", None, "narrow"), P("wide", None, None), P(), P())
    return jax.shard_map(
        per_device,
        mesh=mesh,
        in_specs=placed,
        out_specs=(P("wide", "narrow", None), P("wide", "narrow", None)),
        check_vma=False,
    )
```

profile of v0, /device:TPU:2, one launch (start us, length us, event | category | flops | bytes accessed | tf_op | source)
XLA Modules:
  0.0 966.5 jit_solution(3870654779187750146)
XLA Ops:
  8.0 5.5 fusion.14
  15.3 12.0 %all-to-all-start = ((f32[2,16,64,128]{3,0,1,2:T(2,128)}), f32[2,16,64,128]{3,0,1,2:T(2,128)S(1)}, u32[]{:S(2)}, u32[]{:S(2)}) async-start(f32[2,16,64,128]{3,0,1,2:T(2,128)} %copy.24), calls=%async_computation | async-start | bytes 2097152 | tf_op jit(solution)/shard_map/all_to_all | solution.py:41
  27.4 35.0 %cosine_multiply_fusion = (f32[1,1024,2048]{1,2,0:T(8,128)}, f32[1,1024,2048]{1,2,0:T(8,128)}) fusion(s32[1024]{0:T(1024)S(1)} %copy-done.7, f32[1024]{0:T(1024)S(1)} %get-tuple-element.68, f32[1024]{0:T(1024)S(1)} %get-tuple-element.69), kind=kLoop, calls=%fused_computation.17 | loop fusion | flops 33554432 | bytes 16789504 | tf_op jit(solution)/shard_map/mul | solution.py:38
  62.4 16.5 %fusion = f32[2048,128,1]{1,0,2:T(8,128)S(1)} fusion(f32[2,1024,128]{2,1,0:T(8,128)S(1)} %bitcast.179, f32[1,1024,2048]{1,2,0:T(8,128)} %get-tuple-element.67, f32[1,1024,2048]{1,2,0:T(8,128)} %get-tuple-element.66), kind=kOutput, calls=%fused_computation.4 | convolution fusion | flops 6446645248 | bytes 18874368 | tf_op jit(solution)/shard_map/ksrc,ksj->rjc/dot_general | solution.py:39
  79.0 19.9 %all_to_all.30 = f32[1,2048,128]{2,0,1:T(1,128)S(1)} all-to-all(f32[1,2048,128]{2,0,1:T(1,128)S(1)} %bitcast.180), channel_id=1, replica_groups=mesh['wide'=64,'narrow'=4] {'narrow'}, dimensions={1} | all-to-all | bytes 2097152 | tf_op jit(solution)/shard_map/all_to_all | solution.py:46
  99.7 2.8 fusion.143
  104.0 256.8 %all-reduce.4.cloned.1.call-done = f32[512,512]{0,1:T(8,128)} async-done(((f32[512,512]{0,1:T(8,128)}), f32[512,512]{0,1:T(8,128)}) %all-reduce.4.cloned.1.call-update) | async-done | bytes 1048592 | tf_op jit(solution)/shard_map/psum | solution.py:57
  368.8 11.7 %cholesky.286 = f32[128,128]{1,0:T(8,128)S(1)} custom-call(f32[128,128]{1,0:T(8,128)S(1)} %cholesky.426), custom_call_target="Cholesky" | custom-call | tf_op jit(solution)/shard_map/jit(cholesky)/cholesky | solution.py:18
  380.5 9.8 %custom-call.29 = f32[1,128,128]{1,2,0:T(8,128)S(1)} custom-call(f32[1,128,128]{2,1,0:T(8,128)S(1)} %get-tuple-element.65), custom_call_target="InvertDiagBlocksLowerTriangular" | custom-call | tf_op jit(solution)/shard_map/jit(cholesky)/cholesky | solution.py:18
  393.0 11.7 %cholesky.305 = f32[128,128]{1,0:T(8,128)S(1)} custom-call(f32[128,128]{1,0:T(8,128)S(1)} %cholesky.430), custom_call_target="Cholesky" | custom-call | tf_op jit(solution)/shard_map/jit(cholesky)/cholesky | solution.py:18
  404.7 18.5 %custom-call.30 = f32[1,128,128]{1,2,0:T(8,128)S(1)} custom-call(f32[1,128,128]{2,1,0:T(8,128)S(1)} %get-tuple-element.62), custom_call_target="InvertDiagBlocksLowerTriangular" | custom-call | tf_op jit(solution)/shard_map/jit(cholesky)/cholesky | solution.py:18
  424.8 11.7 %cholesky.326 = f32[128,128]{1,0:T(8,128)S(1)} custom-call(f32[128,128]{1,0:T(8,128)S(1)} %cholesky.435), custom_call_target="Cholesky" | custom-call | tf_op jit(solution)/shard_map/jit(cholesky)/cholesky | solution.py:18
  437.2 9.8 %custom-call.31 = f32[1,128,128]{1,2,0:T(8,128)S(1)} custom-call(f32[1,128,128]{2,1,0:T(8,128)S(1)} %get-tuple-element.59), custom_call_target="InvertDiagBlocksLowerTriangular" | custom-call | tf_op jit(solution)/shard_map/jit(cholesky)/cholesky | solution.py:18
  448.5 12.1 %cholesky.343 = f32[128,128]{1,0:T(8,128)S(1)} custom-call(f32[128,128]{1,0:T(8,128)S(1)} %convolution_subtract_fusion.18), custom_call_target="Cholesky" | custom-call | tf_op jit(solution)/shard_map/jit(cholesky)/cholesky | solution.py:18
  465.6 11.2 %while.4 = (s32[]{:T(128)}, f32[512,512]{1,0:T(8,128)}, s32[4,2]{0,1:T(2,128)S(1)}, f32[4,128,128]{2,1,0:T(8,128)S(1)}, s32[]{:T(128)}) while((s32[]{:T(128)}, f32[512,512]{1,0:T(8,128)}, s32[4,2]{0,1:T(2,128)S(1)}, f32[4,128,128]{2,1,0:T(8,128)S(1)}, s32[]{:T(128)}) %tuple.61), condition=%wide.while_cond, body=%wide.while_body.sunk | while | flops 2 | bytes 131181 | solution.py:21
  477.6 40.1 %custom-call.32 = f32[4,128,128]{1,2,0:T(8,128)S(1)} custom-call(f32[4,128,128]{2,1,0:T(8,128)} %copy-done.5), custom_call_target="InvertDiagBlocksLowerTriangular" | custom-call | tf_op jit(solution)/shard_map/jit(_cho_solve)/triangular_solve | solution.py:21
  522.3 2.4 convolution_subtract_fusion.12
  530.9 3.3 bitcast_subtract_fusion
  534.2 2.9 fusion.144
  537.1 2.5 copy.39
  539.6 255.4 %all-reduce.6.cloned.1.call-done = f32[512,512]{0,1:T(8,128)} async-done(((f32[512,512]{0,1:T(8,128)}), f32[512,512]{0,1:T(8,128)}) %all-reduce.6.cloned.1.call-update) | async-done | bytes 1048592 | tf_op jit(solution)/shard_map/psum | solution.py:57
  803.1 11.9 %cholesky.358 = f32[128,128]{1,0:T(8,128)S(1)} custom-call(f32[128,128]{1,0:T(8,128)S(1)} %cholesky.439), custom_call_target="Cholesky" | custom-call | tf_op jit(solution)/shard_map/jit(cholesky)/cholesky | solution.py:18
  815.1 9.8 %custom-call.33 = f32[1,128,128]{1,2,0:T(8,128)S(1)} custom-call(f32[1,128,128]{2,1,0:T(8,128)S(1)} %get-tuple-element.55), custom_call_target="InvertDiagBlocksLowerTriangular" | custom-call | tf_op jit(solution)/shard_map/jit(cholesky)/cholesky | solution.py:18
  827.5 11.7 %cholesky.377 = f32[128,128]{1,0:T(8,128)S(1)} custom-call(f32[128,128]{1,0:T(8,128)S(1)} %cholesky.443), custom_call_target="Cholesky" | custom-call | tf_op jit(solution)/shard_map/jit(cholesky)/cholesky | solution.py:18
  840.6 10.0 %custom-call.34 = f32[1,128,128]{1,2,0:T(8,128)S(1)} custom-call(f32[1,128,128]{2,1,0:T(8,128)S(1)} %get-tuple-element.52), custom_call_target="InvertDiagBlocksLowerTriangular" | custom-call | tf_op jit(solution)/shard_map/jit(cholesky)/cholesky | solution.py:18
  852.1 11.7 %cholesky.398 = f32[128,128]{1,0:T(8,128)S(1)} custom-call(f32[128,128]{1,0:T(8,128)S(1)} %cholesky.448), custom_call_target="Cholesky" | custom-call | tf_op jit(solution)/shard_map/jit(cholesky)/cholesky | solution.py:18
  864.5 9.8 %custom-call.35 = f32[1,128,128]{1,2,0:T(8,128)S(1)} custom-call(f32[1,128,128]{2,1,0:T(8,128)S(1)} %get-tuple-element.49), custom_call_target="InvertDiagBlocksLowerTriangular" | custom-call | tf_op jit(solution)/shard_map/jit(cholesky)/cholesky | solution.py:18
  875.8 11.7 %cholesky.415 = f32[128,128]{1,0:T(8,128)S(1)} custom-call(f32[128,128]{1,0:T(8,128)S(1)} %convolution_subtract_fusion.17), custom_call_target="Cholesky" | custom-call | tf_op jit(solution)/shard_map/jit(cholesky)/cholesky | solution.py:18
  891.8 11.7 %while.5 = (s32[]{:T(128)}, f32[512,512]{1,0:T(8,128)}, s32[4,2]{0,1:T(2,128)S(1)}, f32[4,128,128]{2,1,0:T(8,128)S(1)}, s32[]{:T(128)}) while((s32[]{:T(128)}, f32[512,512]{1,0:T(8,128)}, s32[4,2]{0,1:T(2,128)S(1)}, f32[4,128,128]{2,1,0:T(8,128)S(1)}, s32[]{:T(128)}) %tuple.71), condition=%wide.while_cond.clone, body=%wide.while_body.clone.sunk | while | flops 2 | bytes 131181 | solution.py:21
  903.6 39.6 %custom-call.36 = f32[4,128,128]{1,2,0:T(8,128)S(1)} custom-call(f32[4,128,128]{2,1,0:T(8,128)S(1)} %get-tuple-element.19), custom_call_target="InvertDiagBlocksLowerTriangular" | custom-call | tf_op jit(solution)/shard_map/jit(_cho_solve)/triangular_solve | solution.py:21
  947.8 2.4 convolution_subtract_fusion.10
  956.3 2.8 convolution_bitcast_fusion
  (128 shorter events, 83.0 us)
Async XLA Ops:
  8.0 19.3 %copy-start.7 = (s32[1024]{0:T(1024)S(1)}, s32[1024]{0:T(1024)}, u32[]{:S(2)}) copy-start(s32[1024]{0:T(1024)} %param.9) | copy-start | bytes 12292
  15.3 47.1 %all-to-all-start = ((f32[2,16,64,128]{3,0,1,2:T(2,128)}), f32[2,16,64,128]{3,0,1,2:T(2,128)S(1)}, u32[]{:S(2)}, u32[]{:S(2)}) async-start(f32[2,16,64,128]{3,0,1,2:T(2,128)} %copy.24), calls=%async_computation | async-start | bytes 2097152 | tf_op jit(solution)/shard_map/all_to_all | solution.py:41
  27.3 333.4 %all-reduce.4.cloned.1.call-start = ((), (), s32[]{:S(2)}) async-start(), calls=%async_computation.2 | async-start | bytes 2097152 | tf_op jit(solution)/shard_map/psum | solution.py:57
  62.4 36.8 %copy-start.6 = (f32[512]{0:T(512)S(1)}, f32[512]{0:T(512)}, u32[]{:S(2)}) copy-start(f32[512]{0:T(512)} %param.10) | copy-start | bytes 6148
  102.5 692.5 %all-reduce.6.cloned.1.call-start = ((), (), s32[]{:S(2)}) async-start(), calls=%async_computation.3 | async-start | bytes 2097152 | tf_op jit(solution)/shard_map/psum | solution.py:57
  360.7 157.0 %copy-start = (f32[512,512]{0,1:T(8,128)S(1)}, f32[512,512]{0,1:T(8,128)}, u32[]{:S(2)}) copy-start(f32[512,512]{0,1:T(8,128)} %all-reduce.4.cloned.1.call-done) | copy-start | bytes 3145732
  367.8 1.0 copy-start.4
  465.6 65.4 %copy-start.2 = (f32[512,512]{0,1:T(8,128)S(1)}, f32[512,512]{0,1:T(8,128)}, u32[]{:S(2)}) copy-start(f32[512,512]{0,1:T(8,128)} %bitcast_subtract_fusion.1) | copy-start | bytes 3145732
  476.8 0.7 copy-start.5
  795.1 148.1 %copy-start.1 = (f32[512,512]{0,1:T(8,128)S(1)}, f32[512,512]{0,1:T(8,128)}, u32[]{:S(2)}) copy-start(f32[512,512]{0,1:T(8,128)} %all-reduce.6.cloned.1.call-done) | copy-start | bytes 3145732
  802.1 1.0 copy-start.3
Sparse Core Ops, SparseCore 0:
  102.6 258.0 all-reduce.3
  537.2 257.7 all-reduce.5
where the time goes:
time: 975 us; the launch traced here: 966 us
  waiting for transfers between devices  512 us (53%)
  other arithmetic  296 us (30%)
  matrix products  71 us (7%)
  local copies, waits for them, and re-layouts  33.9 us (3%)
  between operations  21.4 us (2%)
  blocking collectives  19.9 us (2%)
  starting transfers between devices  12.1 us (1%)
    psum x2, waiting for transfers between devices, per_device(): covariance = lax.psum(partial_cov, ('wide', 'narrow'))  512 us
    another operation x29, other arithmetic, wiener_filter(): jnp.linalg.cholesky(covariance + ridge_shift * jnp.eye(chan_total, dtype=...  167 us
    another operation x5, other arithmetic, wiener_filter(): return jax.scipy.linalg.cho_solve((factor, True), covariance)  81.9 us
    mul x1, other arithmetic, per_device(): weights * jnp.cos(pixel_angle)  35 us
    another operation x28, matrix products, wiener_filter(): return jax.scipy.linalg.cho_solve((factor, True), covariance)  26.2 us
    another operation x27, local copies, waits for them, and re-layouts, wiener_filter(): return jax.scipy.linalg.cho_solve((factor, True), covariance)  22.8 us
    all_to_all x1, blocking collectives, per_device(): lax.all_to_all(sky_map, 'narrow', split_axis=1, concat_axis=2, tiled=True)  19.9 us
  transfers between devices with their start and end apart: 3, of which 2 were waited for; matrix products, arithmetic and copies ran while one was open for 4% of the time, Pallas kernels for 0%

commit v1 on v0

--- a/solution.py
+++ b/solution.py
@@ -54,7 +54,9 @@
         partial_cov = jnp.dot(
             residue.T, residue, precision=lax.Precision.HIGHEST, preferred_element_type=jnp.float32
         )
-        covariance = lax.psum(partial_cov, ("wide", "narrow"))
+        covariance = partial_cov
+        for dd in ("narrow", "wide"):
+            covariance = lax.psum(covariance, axis_name=dd)
         lowrank = jnp.dot(
             residue,
             wiener_filter(covariance),

time: 975 us -> 941 us (0.965)
  waiting for transfers between devices: 512 us -> 477 us
    psum x2 -> x4, waiting for transfers between devices: 512 us -> 477 us  [per_device(): covariance = lax.psum(covariance, axis_name=dd)]
  transfers between devices with their start and end apart: 3 -> 5, of which waited for: 2 -> 4; matrix products, arithmetic and copies ran while one was open for 4% -> 4% of each run, Pallas kernels for 0% -> 0%
where the time goes in v1:
time: 941 us; the launch traced here: 932 us
  waiting for transfers between devices  477 us (51%)
  other arithmetic  296 us (31%)
  matrix products  70.9 us (8%)
  local copies, waits for them, and re-layouts  34.3 us (4%)
  between operations  21.2 us (2%)
  blocking collectives  19.9 us (2%)
  starting transfers between devices  12.3 us (1%)
    psum x4, waiting for transfers between devices, per_device(): covariance = lax.psum(covariance, axis_name=dd)  477 us
    another operation x29, other arithmetic, wiener_filter(): jnp.linalg.cholesky(covariance + ridge_shift * jnp.eye(chan_total, dtype=...  167 us
    another operation x5, other arithmetic, wiener_filter(): return jax.scipy.linalg.cho_solve((factor, True), covariance)  81.6 us
    mul x1, other arithmetic, per_device(): weights * jnp.cos(pixel_angle)  35 us
    another operation x28, matrix products, wiener_filter(): return jax.scipy.linalg.cho_solve((factor, True), covariance)  26.2 us
    another operation x27, local copies, waits for them, and re-layouts, wiener_filter(): return jax.scipy.linalg.cho_solve((factor, True), covariance)  23.3 us
    all_to_all x1, blocking collectives, per_device(): lax.all_to_all(sky_map, 'narrow', split_axis=1, concat_axis=2, tiled=True)  19.9 us
  transfers between devices with their start and end apart: 5, of which 4 were waited for; matrix products, arithmetic and copies ran while one was open for 4% of the time, Pallas kernels for 0%

profile of v1, /device:TPU:2, one launch (start us, length us, event | category | flops | bytes accessed | tf_op | source)
XLA Modules:
  0.0 931.9 jit_solution(15211154648451930842)
XLA Ops:
  8.0 5.5 fusion.14
  15.3 12.0 %all-to-all-start = ((f32[2,16,64,128]{3,0,1,2:T(2,128)}), f32[2,16,64,128]{3,0,1,2:T(2,128)S(1)}, u32[]{:S(2)}, u32[]{:S(2)}) async-start(f32[2,16,64,128]{3,0,1,2:T(2,128)} %copy.24), calls=%async_computation | async-start | bytes 2097152 | tf_op jit(solution)/shard_map/all_to_all | solution.py:41
  27.4 35.0 %cosine_multiply_fusion = (f32[1,1024,2048]{1,2,0:T(8,128)}, f32[1,1024,2048]{1,2,0:T(8,128)}) fusion(s32[1024]{0:T(1024)S(1)} %copy-done.7, f32[1024]{0:T(1024)S(1)} %get-tuple-element.68, f32[1024]{0:T(1024)S(1)} %get-tuple-element.69), kind=kLoop, calls=%fused_computation.17 | loop fusion | flops 33554432 | bytes 16789504 | tf_op jit(solution)/shard_map/mul | solution.py:38
  62.4 16.5 %fusion = f32[2048,128,1]{1,0,2:T(8,128)S(1)} fusion(f32[2,1024,128]{2,1,0:T(8,128)S(1)} %bitcast.179, f32[1,1024,2048]{1,2,0:T(8,128)} %get-tuple-element.67, f32[1,1024,2048]{1,2,0:T(8,128)} %get-tuple-element.66), kind=kOutput, calls=%fused_computation.4 | convolution fusion | flops 6446645248 | bytes 18874368 | tf_op jit(solution)/shard_map/ksrc,ksj->rjc/dot_general | solution.py:39
  79.0 19.9 %all_to_all.30 = f32[1,2048,128]{2,0,1:T(1,128)S(1)} all-to-all(f32[1,2048,128]{2,0,1:T(1,128)S(1)} %bitcast.180), channel_id=1, replica_groups=mesh['wide'=64,'narrow'=4] {'narrow'}, dimensions={1} | all-to-all | bytes 2097152 | tf_op jit(solution)/shard_map/all_to_all | solution.py:46
  99.7 2.8 fusion.143
  102.6 50.6 %all-reduce.6.cloned.1.call-done = f32[512,512]{0,1:T(8,128)} async-done(((f32[512,512]{0,1:T(8,128)}), f32[512,512]{0,1:T(8,128)}) %all-reduce.6.cloned.1.call-update) | async-done | bytes 1048592 | tf_op jit(solution)/shard_map/psum | solution.py:59
  154.6 189.8 %all-reduce.8.cloned.1.call-done = f32[512,512]{0,1:T(8,128)} async-done(((f32[512,512]{0,1:T(8,128)}), f32[512,512]{0,1:T(8,128)}) %all-reduce.8.cloned.1.call-update) | async-done | bytes 1048592 | tf_op jit(solution)/shard_map/psum | solution.py:59
  352.5 11.7 %cholesky.286 = f32[128,128]{1,0:T(8,128)S(1)} custom-call(f32[128,128]{1,0:T(8,128)S(1)} %cholesky.426), custom_call_target="Cholesky" | custom-call | tf_op jit(solution)/shard_map/jit(cholesky)/cholesky | solution.py:18
  364.2 9.8 %custom-call.29 = f32[1,128,128]{1,2,0:T(8,128)S(1)} custom-call(f32[1,128,128]{2,1,0:T(8,128)S(1)} %get-tuple-element.65), custom_call_target="InvertDiagBlocksLowerTriangular" | custom-call | tf_op jit(solution)/shard_map/jit(cholesky)/cholesky | solution.py:18
  376.7 11.7 %cholesky.305 = f32[128,128]{1,0:T(8,128)S(1)} custom-call(f32[128,128]{1,0:T(8,128)S(1)} %cholesky.430), custom_call_target="Cholesky" | custom-call | tf_op jit(solution)/shard_map/jit(cholesky)/cholesky | solution.py:18
  388.4 18.5 %custom-call.30 = f32[1,128,128]{1,2,0:T(8,128)S(1)} custom-call(f32[1,128,128]{2,1,0:T(8,128)S(1)} %get-tuple-element.62), custom_call_target="InvertDiagBlocksLowerTriangular" | custom-call | tf_op jit(solution)/shard_map/jit(cholesky)/cholesky | solution.py:18
  408.5 11.7 %cholesky.326 = f32[128,128]{1,0:T(8,128)S(1)} custom-call(f32[128,128]{1,0:T(8,128)S(1)} %cholesky.435), custom_call_target="Cholesky" | custom-call | tf_op jit(solution)/shard_map/jit(cholesky)/cholesky | solution.py:18
  421.0 9.8 %custom-call.31 = f32[1,128,128]{1,2,0:T(8,128)S(1)} custom-call(f32[1,128,128]{2,1,0:T(8,128)S(1)} %get-tuple-element.59), custom_call_target="InvertDiagBlocksLowerTriangular" | custom-call | tf_op jit(solution)/shard_map/jit(cholesky)/cholesky | solution.py:18
  432.3 12.1 %cholesky.343 = f32[128,128]{1,0:T(8,128)S(1)} custom-call(f32[128,128]{1,0:T(8,128)S(1)} %convolution_subtract_fusion.18), custom_call_target="Cholesky" | custom-call | tf_op jit(solution)/shard_map/jit(cholesky)/cholesky | solution.py:18
  449.4 11.7 %while.4 = (s32[]{:T(128)}, f32[512,512]{1,0:T(8,128)}, s32[4,2]{0,1:T(2,128)S(1)}, f32[4,128,128]{2,1,0:T(8,128)S(1)}, s32[]{:T(128)}) while((s32[]{:T(128)}, f32[512,512]{1,0:T(8,128)}, s32[4,2]{0,1:T(2,128)S(1)}, f32[4,128,128]{2,1,0:T(8,128)S(1)}, s32[]{:T(128)}) %tuple.61), condition=%wide.while_cond, body=%wide.while_body.sunk | while | flops 2 | bytes 131181 | solution.py:21
  461.8 40.1 %custom-call.32 = f32[4,128,128]{1,2,0:T(8,128)S(1)} custom-call(f32[4,128,128]{2,1,0:T(8,128)} %copy-done.5), custom_call_target="InvertDiagBlocksLowerTriangular" | custom-call | tf_op jit(solution)/shard_map/jit(_cho_solve)/triangular_solve | solution.py:21
  515.1 3.3 bitcast_subtract_fusion
  518.4 2.8 fusion.144
  521.5 48.4 %all-reduce.10.cloned.1.call-done = f32[512,512]{0,1:T(8,128)} async-done(((f32[512,512]{0,1:T(8,128)}), f32[512,512]{0,1:T(8,128)}) %all-reduce.10.cloned.1.call-update) | async-done | bytes 1048592 | tf_op jit(solution)/shard_map/psum | solution.py:59
  569.9 2.5 copy.39
  572.4 188.6 %all-reduce.12.cloned.1.call-done = f32[512,512]{0,1:T(8,128)} async-done(((f32[512,512]{0,1:T(8,128)}), f32[512,512]{0,1:T(8,128)}) %all-reduce.12.cloned.1.call-update) | async-done | bytes 1048592 | tf_op jit(solution)/shard_map/psum | solution.py:59
  769.0 11.7 %cholesky.358 = f32[128,128]{1,0:T(8,128)S(1)} custom-call(f32[128,128]{1,0:T(8,128)S(1)} %cholesky.439), custom_call_target="Cholesky" | custom-call | tf_op jit(solution)/shard_map/jit(cholesky)/cholesky | solution.py:18
  780.9 9.8 %custom-call.33 = f32[1,128,128]{1,2,0:T(8,128)S(1)} custom-call(f32[1,128,128]{2,1,0:T(8,128)S(1)} %get-tuple-element.55), custom_call_target="InvertDiagBlocksLowerTriangular" | custom-call | tf_op jit(solution)/shard_map/jit(cholesky)/cholesky | solution.py:18
  793.2 11.7 %cholesky.377 = f32[128,128]{1,0:T(8,128)S(1)} custom-call(f32[128,128]{1,0:T(8,128)S(1)} %cholesky.443), custom_call_target="Cholesky" | custom-call | tf_op jit(solution)/shard_map/jit(cholesky)/cholesky | solution.py:18
  806.3 10.0 %custom-call.34 = f32[1,128,128]{1,2,0:T(8,128)S(1)} custom-call(f32[1,128,128]{2,1,0:T(8,128)S(1)} %get-tuple-element.52), custom_call_target="InvertDiagBlocksLowerTriangular" | custom-call | tf_op jit(solution)/shard_map/jit(cholesky)/cholesky | solution.py:18
  817.9 11.7 %cholesky.398 = f32[128,128]{1,0:T(8,128)S(1)} custom-call(f32[128,128]{1,0:T(8,128)S(1)} %cholesky.448), custom_call_target="Cholesky" | custom-call | tf_op jit(solution)/shard_map/jit(cholesky)/cholesky | solution.py:18
  830.3 9.8 %custom-call.35 = f32[1,128,128]{1,2,0:T(8,128)S(1)} custom-call(f32[1,128,128]{2,1,0:T(8,128)S(1)} %get-tuple-element.49), custom_call_target="InvertDiagBlocksLowerTriangular" | custom-call | tf_op jit(solution)/shard_map/jit(cholesky)/cholesky | solution.py:18
  841.6 11.9 %cholesky.415 = f32[128,128]{1,0:T(8,128)S(1)} custom-call(f32[128,128]{1,0:T(8,128)S(1)} %convolution_subtract_fusion.17), custom_call_target="Cholesky" | custom-call | tf_op jit(solution)/shard_map/jit(cholesky)/cholesky | solution.py:18
  857.9 11.7 %while.5 = (s32[]{:T(128)}, f32[512,512]{1,0:T(8,128)}, s32[4,2]{0,1:T(2,128)S(1)}, f32[4,128,128]{2,1,0:T(8,128)S(1)}, s32[]{:T(128)}) while((s32[]{:T(128)}, f32[512,512]{1,0:T(8,128)}, s32[4,2]{0,1:T(2,128)S(1)}, f32[4,128,128]{2,1,0:T(8,128)S(1)}, s32[]{:T(128)}) %tuple.75), condition=%wide.while_cond.clone, body=%wide.while_body.clone.sunk | while | flops 2 | bytes 131181 | solution.py:21
  869.6 39.3 %custom-call.36 = f32[4,128,128]{1,2,0:T(8,128)S(1)} custom-call(f32[4,128,128]{2,1,0:T(8,128)S(1)} %get-tuple-element.19), custom_call_target="InvertDiagBlocksLowerTriangular" | custom-call | tf_op jit(solution)/shard_map/jit(_cho_solve)/triangular_solve | solution.py:21
  922.1 2.8 convolution_bitcast_fusion
  (134 shorter events, 88.6 us)
Async XLA Ops:
  8.0 19.3 %copy-start.7 = (s32[1024]{0:T(1024)S(1)}, s32[1024]{0:T(1024)}, u32[]{:S(2)}) copy-start(s32[1024]{0:T(1024)} %param.9) | copy-start | bytes 12292
  15.3 47.1 %all-to-all-start = ((f32[2,16,64,128]{3,0,1,2:T(2,128)}), f32[2,16,64,128]{3,0,1,2:T(2,128)S(1)}, u32[]{:S(2)}, u32[]{:S(2)}) async-start(f32[2,16,64,128]{3,0,1,2:T(2,128)} %copy.24), calls=%async_computation | async-start | bytes 2097152 | tf_op jit(solution)/shard_map/all_to_all | solution.py:41
  27.3 125.9 %all-reduce.6.cloned.1.call-start = ((), (), s32[]{:S(2)}) async-start(), calls=%async_computation.2 | async-start | bytes 2097152 | tf_op jit(solution)/shard_map/psum | solution.py:59
  62.4 36.8 %copy-start.6 = (f32[512]{0:T(512)S(1)}, f32[512]{0:T(512)}, u32[]{:S(2)}) copy-start(f32[512]{0:T(512)} %param.10) | copy-start | bytes 6148
  102.5 241.9 %all-reduce.8.cloned.1.call-start = ((), (), s32[]{:S(2)}) async-start(), calls=%async_computation.3 | async-start | bytes 2097152 | tf_op jit(solution)/shard_map/psum | solution.py:59
  153.2 416.7 %all-reduce.10.cloned.1.call-start = ((), (), s32[]{:S(2)}) async-start(), calls=%async_computation.4 | async-start | bytes 2097152 | tf_op jit(solution)/shard_map/psum | solution.py:59
  344.4 157.5 %copy-start = (f32[512,512]{0,1:T(8,128)S(1)}, f32[512,512]{0,1:T(8,128)}, u32[]{:S(2)}) copy-start(f32[512,512]{0,1:T(8,128)} %all-reduce.8.cloned.1.call-done) | copy-start | bytes 3145732
  351.5 1.0 copy-start.4
  449.3 65.8 %copy-start.2 = (f32[512,512]{0,1:T(8,128)S(1)}, f32[512,512]{0,1:T(8,128)}, u32[]{:S(2)}) copy-start(f32[512,512]{0,1:T(8,128)} %bitcast_subtract_fusion.1) | copy-start | bytes 3145732
  461.1 0.7 copy-start.5
  521.3 239.7 %all-reduce.12.cloned.1.call-start = ((), (), s32[]{:S(2)}) async-start(), calls=%async_computation.5 | async-start | bytes 2097152 | tf_op jit(solution)/shard_map/psum | solution.py:59
  761.0 147.9 %copy-start.1 = (f32[512,512]{0,1:T(8,128)S(1)}, f32[512,512]{0,1:T(8,128)}, u32[]{:S(2)}) copy-start(f32[512,512]{0,1:T(8,128)} %all-reduce.12.cloned.1.call-done) | copy-start | bytes 3145732
  768.0 1.0 copy-start.3
Sparse Core Ops, SparseCore 0:
  102.6 50.4 all-reduce.5
  156.6 187.8 all-reduce.7
  521.4 48.4 all-reduce.9
  573.1 187.7 all-reduce.11
